TPU v7x, 32 devices: a whole 2x2x4 slice. The times are simulated.
32 devices in a mesh: groups: 2 (over x), blk: 8 (over z, y), split: 2 (over core).
Axes of the slice: x: 2, y: 2, z: 4, core: 2. Of those that a mesh axis runs over, the one named last changes fastest.
Arguments:
- embeddings: bfloat16 [32768, 768], P(('groups', 'blk', 'split')), parts along dimension 0, may hold values from -6 to 6
- cluster_of: int32 [32768], P(('groups', 'blk', 'split')), parts along dimension 0, may hold values from 0 to 15, as said below
- target_pos: int32 [32768], P(('groups', 'blk', 'split')), parts along dimension 0, may hold values from 0 to 16383, as said below
Outputs:
- best: float32 [32768], P(('groups', 'blk', 'split')), parts along dimension 0
There are 2 independent parts, one for each index of `groups`. A program takes and returns all parts, laid end to end along the dimension named above; each array names one. Nothing has to cross between parts.
Inputs may be any that keep to these rules, and one draw needn't show every extreme that they name: `cluster_of`: ordering the members by target_pos lists cluster 0 first, then cluster 1 and so on, each cluster's members contiguous; every cluster has 2 to 4096 members and one has exactly 4096. `target_pos`: A permutation of the rows. For every aligned block of 1024 positions, each device's 1024 data-order rows hold exactly 64 of its positions.
All inputs are finite; a program needn't handle non-finite values.
Results may differ from a plain program's by a relative error of at most 0.0025.
Values may be sent and summed in bfloat16 or wider, within the bound.
A program may use at most 64 MiB of HBM per device.

v0:
```python
import jax
import jax.numpy as jnp
from jax import lax
from jax.sharding import PartitionSpec as P

MOST = 4096
FILL = -4.0


def from_behind(block, axis, distance):
    devices = range(lax.axis_size(axis))
    route = [((i - distance) % len(devices), i) for i in devices]
    return lax.ppermute(block, axis, route)


def masked_scores(left, left_ids, right, right_ids):
    sims = lax.dot_general(
        left, right, (((1,), (1,)), ((), ())), preferred_element_type=jnp.float32
    )
    return jnp.where(left_ids[:, None] == right_ids[None, :], sims, FILL)


def body(embeddings, cluster_of, target_pos):
    count = lax.axis_size(("blk", "split"))
    rows, width = embeddings.shape
    piece = rows // count
    me = lax.axis_index(("blk", "split"))
    values = embeddings.astype(jnp.float32)
    unit = (values * lax.rsqrt(jnp.sum(values * values, axis=1, keepdims=True) + 1e-06)).astype(
        jnp.bfloat16
    )
    order = jnp.argsort(target_pos)
    packed = unit[order].reshape(count, piece, width)
    labels = jnp.stack(
        [cluster_of[order].reshape(count, piece), target_pos[order].reshape(count, piece)], axis=1
    )
    received, tags = (
        lax.all_to_all(packed, ("blk", "split"), split_axis=0, concat_axis=0, tiled=True),
        lax.all_to_all(labels, ("blk", "split"), split_axis=0, concat_axis=0, tiled=True),
    )
    unit_in = received.reshape(rows, width)
    ids_in = tags[:, 0, :].reshape(rows)
    local = tags[:, 1, :].reshape(rows) - me * rows
    place = jnp.argsort(local)
    mine = unit_in[place]
    my_ids = ids_in[place]
    reach = (MOST + rows - 2) // rows
    own = masked_scores(mine, my_ids, mine, my_ids)
    diagonal = jnp.arange(rows)[:, None] == jnp.arange(rows)[None, :]
    best = jnp.max(jnp.where(diagonal, FILL, own), axis=1)

    def both_maxima(pair, visit_unit, visit_ids):
        row_best, visit_best = pair
        scores = masked_scores(mine, my_ids, visit_unit, visit_ids)
        return (
            jnp.maximum(row_best, jnp.max(scores, axis=1)),
            jnp.maximum(visit_best, jnp.max(scores, axis=0)),
        )

    def turn(step, carry):
        row_best, visit_unit, visit_ids, visit_best = carry
        visit_unit, visit_ids, visit_best = (
            from_behind(visit_unit, ("blk", "split"), 1),
            from_behind(visit_ids, ("blk", "split"), 1),
            from_behind(visit_best.astype(jnp.bfloat16), ("blk", "split"), 1).astype(
                visit_best.dtype
            ),
        )
        row_best, visit_best = both_maxima((row_best, visit_best), visit_unit, visit_ids)
        return (row_best, visit_unit, visit_ids, visit_best)

    start_best = jnp.full((rows,), FILL, jnp.float32)
    best, visit_unit, visit_ids, visit_best = lax.fori_loop(
        0, reach, turn, (best, mine, my_ids, start_best)
    )
    returned_home = from_behind(visit_best, ("blk", "split"), -reach)
    best = jnp.maximum(best, returned_home)
    back = best[local].reshape(count, piece)
    returned = lax.all_to_all(
        back, ("blk", "split"), split_axis=0, concat_axis=0, tiled=True
    ).reshape(rows)
    return jnp.zeros((rows,), jnp.float32).at[order].set(returned)


def solution(mesh):
    return jax.shard_map(
        body,
        mesh=mesh,
        in_specs=(
            P(("groups", "blk", "split"), None),
            P(("groups", "blk", "split")),
            P(("groups", "blk", "split")),
        ),
        out_specs=P(("groups", "blk", "split")),
        check_vma=False,
    )
```

profile of v0, /device:TPU:0, one launch (start us, length us, event | category | flops | bytes accessed | tf_op | source)
XLA Modules:
  0.0 204.1 jit_solution(9965459332306292172)
XLA Ops:
  0.0 5.1 %sort.31 = (s32[1024]{0:T(1024)}, s32[1024]{0:T(1024)S(1)}) sort(s32[1024]{0:T(1024)} %param.7, s32[1024]{0:T(1024)S(1)} %iota.15), dimensions={0}, to_apply=%region_0.0 | sort | flops 10240 | bytes 16384 | tf_op jit(solution)/shard_map/jit(argsort)/sort | solution.py:32
  5.1 4.5 %gather_fusion.1 = s32[1024]{0:T(1024)S(1)} fusion(s32[1024]{0:T(1024)S(1)} %copy-done.1, s32[1024]{0:T(1024)S(1)} %get-tuple-element.92), kind=kCustom, calls=%fused_computation.1 | custom fusion | bytes 12288 | tf_op jit(solution)/shard_map/gather | solution.py:35
  9.8 4.5 %gather_fusion = s32[1024]{0:T(1024)S(1)} fusion(s32[1024]{0:T(1024)S(1)} %copy-done, s32[1024]{0:T(1024)S(1)} %get-tuple-element.92), kind=kCustom, calls=%fused_computation | custom fusion | bytes 12288 | tf_op jit(solution)/shard_map/gather | solution.py:35
  15.1 7.4 %all-to-all-start = ((s32[16,1,128]{2,1,0:T(1,128)}), s32[16,1,128]{2,1,0:T(1,128)S(1)}, u32[]{:S(2)}, u32[]{:S(2)}) async-start(s32[16,1,128]{2,1,0:T(1,128)} %reshape.140), calls=%async_computation | async-start | bytes 16384 | tf_op jit(solution)/shard_map/all_to_all | solution.py:39
  23.2 5.2 %gather_fusion.3 = bf16[1024,768]{1,0:T(8,128)(2,1)} fusion(bf16[1024,768]{1,0:T(8,128)(2,1)S(1)} %fusion.3, s32[1024]{0:T(1024)S(1)} %get-tuple-element.92), kind=kCustom, calls=%fused_computation.3 | custom fusion | bytes 3149824 | tf_op jit(solution)/shard_map/gather | solution.py:33
  28.9 5.5 %all-to-all-start.1 = ((bf16[16,64,768]{2,1,0:T(8,128)(2,1)}), bf16[16,64,768]{2,1,0:T(8,128)(2,1)S(1)}, u32[]{:S(2)}, u32[]{:S(2)}) async-start(bf16[16,64,768]{2,1,0:T(8,128)(2,1)} %bitcast), calls=%async_computation.1 | async-start | bytes 3145728 | tf_op jit(solution)/shard_map/all_to_all | solution.py:38
  37.2 4.4 %sort.32 = (s32[1024]{0:T(1024)}, s32[1024]{0:T(1024)S(1)}) sort(s32[1024]{0:T(1024)S(1)} %sub.21, s32[1024]{0:T(1024)S(1)} %iota.16), dimensions={0}, to_apply=%region_1.0 | sort | flops 10240 | bytes 16384 | tf_op jit(solution)/shard_map/jit(argsort)/sort | solution.py:44
  41.6 4.5 %gather_fusion.2 = s32[1024]{0:T(1024)S(1)} fusion(s32[1024]{0:T(1024)S(1)} %reshape_squeeze.4, s32[1024]{0:T(1024)S(1)} %fusion.4), kind=kCustom, calls=%fused_computation.2 | custom fusion | bytes 12288 | tf_op jit(solution)/shard_map/gather | solution.py:46
  46.1 20.2 %all-to-all-done.1 = bf16[16,64,768]{2,1,0:T(8,128)(2,1)S(1)} async-done(((bf16[16,64,768]{2,1,0:T(8,128)(2,1)}), bf16[16,64,768]{2,1,0:T(8,128)(2,1)S(1)}, u32[]{:S(2)}, u32[]{:S(2)}) %all-to-all-start.1) | async-done | bytes 1572896 | tf_op jit(solution)/shard_map/all_to_all | solution.py:38
  66.3 4.0 %gather_fusion.4 = bf16[1024,768]{1,0:T(8,128)(2,1)S(1)} fusion(bf16[1024,768]{1,0:T(8,128)(2,1)S(1)} %bitcast.13, s32[1024]{0:T(1024)S(1)} %fusion.4), kind=kCustom, calls=%fused_computation.4 | custom fusion | bytes 3149824 | tf_op jit(solution)/shard_map/gather | solution.py:45
  70.3 1.8 select_reduce_fusion
  72.1 1.2 copy.6
  73.3 107.0 %while.17 = (s32[]{:T(128)}, f32[1024]{0:T(1024)S(1)}, bf16[1024,768]{1,0:T(8,128)(2,1)}, s32[1024]{0:T(1024)S(1)}, f32[1024]{0:T(1024)S(1)}, /*index=5*/s32[102...) while((s32[]{:T(128)}, f32[1024]{0:T(1024)S(1)}, bf16[1024,768]{1,0:T(8,128)(2,1)}, ...), condition=%wide.region_7.8_spmd.clone, body=%wide.region_4.0_spmd.clone.sunk | while | flops 1614809088 | bytes 12660959 | solution.py:73
  73.3 1.0 collective-permute-start.1
  74.3 1.8 collective-permute-start
  76.1 1.0 collective-permute-start.2
  77.1 22.3 %collective-permute-done = s32[1024]{0:T(1024)S(1)} collective-permute-done((s32[1024]{0:T(1024)S(1)}, s32[1024]{0:T(1024)S(1)}, u32[]{:S(2)}, u32[]{:S(2)}) %collective-permute-start) | collective-permute-done | bytes 4128 | tf_op jit(solution)/shard_map/while/body/eval_jaxpr/ppermute | solution.py:13
  99.4 1.9 fusion.17
  101.3 1.2 copy.16
  102.7 22.6 %collective-permute-done = s32[1024]{0:T(1024)S(1)} collective-permute-done((s32[1024]{0:T(1024)S(1)}, s32[1024]{0:T(1024)S(1)}, u32[]{:S(2)}, u32[]{:S(2)}) %collective-permute-start) | collective-permute-done | bytes 4128 | tf_op jit(solution)/shard_map/while/body/eval_jaxpr/ppermute | solution.py:13
  125.3 1.9 fusion.17
  127.2 1.2 copy.16
  128.6 22.6 %collective-permute-done = s32[1024]{0:T(1024)S(1)} collective-permute-done((s32[1024]{0:T(1024)S(1)}, s32[1024]{0:T(1024)S(1)}, u32[]{:S(2)}, u32[]{:S(2)}) %collective-permute-start) | collective-permute-done | bytes 4128 | tf_op jit(solution)/shard_map/while/body/eval_jaxpr/ppermute | solution.py:13
  151.2 1.9 fusion.17
  153.1 1.2 copy.16
  154.5 22.7 %collective-permute-done = s32[1024]{0:T(1024)S(1)} collective-permute-done((s32[1024]{0:T(1024)S(1)}, s32[1024]{0:T(1024)S(1)}, u32[]{:S(2)}, u32[]{:S(2)}) %collective-permute-start) | collective-permute-done | bytes 4128 | tf_op jit(solution)/shard_map/while/body/eval_jaxpr/ppermute | solution.py:13
  177.2 1.9 fusion.17
  179.2 1.2 copy.16
  180.3 3.6 %collective-permute-done.3 = f32[1024]{0:T(1024)S(1)} collective-permute-done((f32[1024]{0:T(1024)S(1)}, f32[1024]{0:T(1024)S(1)}, u32[]{:S(2)}, u32[]{:S(2)}) %collective-permute-start.3) | collective-permute-done | bytes 4128 | tf_op jit(solution)/shard_map/ppermute | solution.py:13
  183.9 4.5 %gather_fusion.5 = f32[1024]{0:T(1024)S(1)} fusion(f32[1024]{0:T(1024)S(1)} %max.9, s32[1024]{0:T(1024)S(1)} %broadcast_clamp_fusion), kind=kCustom, calls=%fused_computation.5 | custom fusion | bytes 12288 | tf_op jit(solution)/shard_map/gather | solution.py:78
  188.5 9.4 %all_to_all.19 = f32[16,1,64]{2,1,0:T(1,128)S(1)} all-to-all(f32[16,1,64]{2,1,0:T(1,128)S(1)} %all_to_all.14), channel_id=1, replica_groups=mesh['groups'=2,'blk'=8,'split'=2] {'blk','split'}, dimensions={0} | all-to-all | bytes 8192 | tf_op jit(solution)/shard_map/all_to_all | solution.py:79
  199.2 4.9 %scatter_custom_fusion = f32[1024]{0:T(1024)} fusion(s32[1024]{0:T(1024)S(1)} %get-tuple-element.93, f32[1024]{0:T(1024)S(1)} %reshape.102, f32[]{:T(128)} %constant.3.clone.1), kind=kCustom, calls=%fused_computation.28 | custom fusion | bytes 4100 | tf_op jit(solution)/shard_map/scatter | solution.py:82
  (69 shorter events, 6.5 us)
Async XLA Ops:
  0.0 9.8 %copy-start = (s32[1024]{0:T(1024)S(1)}, s32[1024]{0:T(1024)}, u32[]{:S(2)}) copy-start(s32[1024]{0:T(1024)} %param.6) | copy-start | bytes 12292
  0.0 5.1 %copy-start.1 = (s32[1024]{0:T(1024)S(1)}, s32[1024]{0:T(1024)}, u32[]{:S(2)}) copy-start(s32[1024]{0:T(1024)} %param.7) | copy-start | bytes 12292
  9.8 12.7 %copy-start.2 = (bf16[1024,768]{1,0:T(8,128)(2,1)S(1)}, bf16[1024,768]{1,0:T(8,128)(2,1)}, u32[]{:S(2)}) copy-start(bf16[1024,768]{1,0:T(8,128)(2,1)} %param.5) | copy-start | bytes 4718596
  15.1 13.8 %all-to-all-start = ((s32[16,1,128]{2,1,0:T(1,128)}), s32[16,1,128]{2,1,0:T(1,128)S(1)}, u32[]{:S(2)}, u32[]{:S(2)}) async-start(s32[16,1,128]{2,1,0:T(1,128)} %reshape.140), calls=%async_computation | async-start | bytes 16384 | tf_op jit(solution)/shard_map/all_to_all | solution.py:39
  28.9 37.4 %all-to-all-start.1 = ((bf16[16,64,768]{2,1,0:T(8,128)(2,1)}), bf16[16,64,768]{2,1,0:T(8,128)(2,1)S(1)}, u32[]{:S(2)}, u32[]{:S(2)}) async-start(bf16[16,64,768]{2,1,0:T(8,128)(2,1)} %bitcast), calls=%async_computation.1 | async-start | bytes 3145728 | tf_op jit(solution)/shard_map/all_to_all | solution.py:38
  73.3 26.1 %collective-permute-start.1 = (bf16[1024,768]{1,0:T(8,128)(2,1)}, bf16[1024,768]{1,0:T(8,128)(2,1)S(1)}, u32[]{:S(2)}, u32[]{:S(2)}) collective-permute-start(bf16[1024,768]{1,0:T(8,128)(2,1)} %get-tuple-element.152), channel_id=1, source_target_pairs={{15,0},{0,1},{1,2},{2,3},{3,4},{4,5},{5,6},{6,7},{7,8},{8,9},{9,10... | collective-permute-start | bytes 4718600 | tf_op jit(solution)/shard_map/while/body/eval_jaxpr/ppermute | solution.py:13
  74.3 25.1 %collective-permute-start = (s32[1024]{0:T(1024)S(1)}, s32[1024]{0:T(1024)S(1)}, u32[]{:S(2)}, u32[]{:S(2)}) collective-permute-start(s32[1024]{0:T(1024)S(1)} %get-tuple-element.153), channel_id=1, source_target_pairs={{15,0},{0,1},{1,2},{2,3},{3,4},{4,5},{5,6},{6,7},{7,8},{8,9},{9,10... | collective-permute-start | bytes 12296 | tf_op jit(solution)/shard_map/while/body/eval_jaxpr/ppermute | solution.py:13
  76.1 26.4 %collective-permute-start.2 = (bf16[1024]{0:T(1024)(128)(2,1)S(1)}, bf16[1024]{0:T(1024)(128)(2,1)S(1)}, u32[]{:S(2)}, u32[]{:S(2)}) collective-permute-start(bf16[1024]{0:T(1024)(128)(2,1)S(1)} %select_convert_fusion.2), channel_id=1, source_target_pairs={{15,0},{0,1},{1,2},{2,3},{3,4},{4,5},{5,6},{6,7},{7,8},{8,9},{9,10... | collective-permute-start | bytes 6152 | tf_op jit(solution)/shard_map/while/body/eval_jaxpr/ppermute | solution.py:13
  102.5 22.8 %collective-permute-start.1 = (bf16[1024,768]{1,0:T(8,128)(2,1)}, bf16[1024,768]{1,0:T(8,128)(2,1)S(1)}, u32[]{:S(2)}, u32[]{:S(2)}) collective-permute-start(bf16[1024,768]{1,0:T(8,128)(2,1)} %get-tuple-element.152), channel_id=1, source_target_pairs={{15,0},{0,1},{1,2},{2,3},{3,4},{4,5},{5,6},{6,7},{7,8},{8,9},{9,10... | collective-permute-start | bytes 4718600 | tf_op jit(solution)/shard_map/while/body/eval_jaxpr/ppermute | solution.py:13
  102.5 22.8 %collective-permute-start = (s32[1024]{0:T(1024)S(1)}, s32[1024]{0:T(1024)S(1)}, u32[]{:S(2)}, u32[]{:S(2)}) collective-permute-start(s32[1024]{0:T(1024)S(1)} %get-tuple-element.153), channel_id=1, source_target_pairs={{15,0},{0,1},{1,2},{2,3},{3,4},{4,5},{5,6},{6,7},{7,8},{8,9},{9,10... | collective-permute-start | bytes 12296 | tf_op jit(solution)/shard_map/while/body/eval_jaxpr/ppermute | solution.py:13
  102.6 25.8 %collective-permute-start.2 = (bf16[1024]{0:T(1024)(128)(2,1)S(1)}, bf16[1024]{0:T(1024)(128)(2,1)S(1)}, u32[]{:S(2)}, u32[]{:S(2)}) collective-permute-start(bf16[1024]{0:T(1024)(128)(2,1)S(1)} %select_convert_fusion.2), channel_id=1, source_target_pairs={{15,0},{0,1},{1,2},{2,3},{3,4},{4,5},{5,6},{6,7},{7,8},{8,9},{9,10... | collective-permute-start | bytes 6152 | tf_op jit(solution)/shard_map/while/body/eval_jaxpr/ppermute | solution.py:13
  128.4 22.8 %collective-permute-start.1 = (bf16[1024,768]{1,0:T(8,128)(2,1)}, bf16[1024,768]{1,0:T(8,128)(2,1)S(1)}, u32[]{:S(2)}, u32[]{:S(2)}) collective-permute-start(bf16[1024,768]{1,0:T(8,128)(2,1)} %get-tuple-element.152), channel_id=1, source_target_pairs={{15,0},{0,1},{1,2},{2,3},{3,4},{4,5},{5,6},{6,7},{7,8},{8,9},{9,10... | collective-permute-start | bytes 4718600 | tf_op jit(solution)/shard_map/while/body/eval_jaxpr/ppermute | solution.py:13
  128.4 22.8 %collective-permute-start = (s32[1024]{0:T(1024)S(1)}, s32[1024]{0:T(1024)S(1)}, u32[]{:S(2)}, u32[]{:S(2)}) collective-permute-start(s32[1024]{0:T(1024)S(1)} %get-tuple-element.153), channel_id=1, source_target_pairs={{15,0},{0,1},{1,2},{2,3},{3,4},{4,5},{5,6},{6,7},{7,8},{8,9},{9,10... | collective-permute-start | bytes 12296 | tf_op jit(solution)/shard_map/while/body/eval_jaxpr/ppermute | solution.py:13
  128.5 25.8 %collective-permute-start.2 = (bf16[1024]{0:T(1024)(128)(2,1)S(1)}, bf16[1024]{0:T(1024)(128)(2,1)S(1)}, u32[]{:S(2)}, u32[]{:S(2)}) collective-permute-start(bf16[1024]{0:T(1024)(128)(2,1)S(1)} %select_convert_fusion.2), channel_id=1, source_target_pairs={{15,0},{0,1},{1,2},{2,3},{3,4},{4,5},{5,6},{6,7},{7,8},{8,9},{9,10... | collective-permute-start | bytes 6152 | tf_op jit(solution)/shard_map/while/body/eval_jaxpr/ppermute | solution.py:13
  154.3 22.9 %collective-permute-start.1 = (bf16[1024,768]{1,0:T(8,128)(2,1)}, bf16[1024,768]{1,0:T(8,128)(2,1)S(1)}, u32[]{:S(2)}, u32[]{:S(2)}) collective-permute-start(bf16[1024,768]{1,0:T(8,128)(2,1)} %get-tuple-element.152), channel_id=1, source_target_pairs={{15,0},{0,1},{1,2},{2,3},{3,4},{4,5},{5,6},{6,7},{7,8},{8,9},{9,10... | collective-permute-start | bytes 4718600 | tf_op jit(solution)/shard_map/while/body/eval_jaxpr/ppermute | solution.py:13
  154.3 22.9 %collective-permute-start = (s32[1024]{0:T(1024)S(1)}, s32[1024]{0:T(1024)S(1)}, u32[]{:S(2)}, u32[]{:S(2)}) collective-permute-start(s32[1024]{0:T(1024)S(1)} %get-tuple-element.153), channel_id=1, source_target_pairs={{15,0},{0,1},{1,2},{2,3},{3,4},{4,5},{5,6},{6,7},{7,8},{8,9},{9,10... | collective-permute-start | bytes 12296 | tf_op jit(solution)/shard_map/while/body/eval_jaxpr/ppermute | solution.py:13
  154.4 25.9 %collective-permute-start.2 = (bf16[1024]{0:T(1024)(128)(2,1)S(1)}, bf16[1024]{0:T(1024)(128)(2,1)S(1)}, u32[]{:S(2)}, u32[]{:S(2)}) collective-permute-start(bf16[1024]{0:T(1024)(128)(2,1)S(1)} %select_convert_fusion.2), channel_id=1, source_target_pairs={{15,0},{0,1},{1,2},{2,3},{3,4},{4,5},{5,6},{6,7},{7,8},{8,9},{9,10... | collective-permute-start | bytes 6152 | tf_op jit(solution)/shard_map/while/body/eval_jaxpr/ppermute | solution.py:13
  180.3 3.6 %collective-permute-start.3 = (f32[1024]{0:T(1024)S(1)}, f32[1024]{0:T(1024)S(1)}, u32[]{:S(2)}, u32[]{:S(2)}) collective-permute-start(f32[1024]{0:T(1024)S(1)} %get-tuple-element.48), channel_id=1, source_target_pairs={{4,0},{5,1},{6,2},{7,3},{8,4},{9,5},{10,6},{11,7},{12,8},{13,9},{1... | collective-permute-start | bytes 12296 | tf_op jit(solution)/shard_map/ppermute | solution.py:13
where the time goes:
time: 204 us
  waiting for transfers between devices  115 us (56%)
  local copies, waits for them, and re-layouts  40.8 us (20%)
  starting transfers between devices  17.1 us (8%)
  other arithmetic  12.3 us (6%)
  matrix products  9.56 us (5%)
  blocking collectives  9.41 us (5%)
    ppermute x13, waiting for transfers between devices, from_behind(): return lax.ppermute(block, axis, route)  93.9 us
    all_to_all x1, waiting for transfers between devices, body(): lax.all_to_all(packed, ('blk', 'split'), split_axis=0, concat_axis=0, til...  20.2 us
    dot_general x5, matrix products, masked_scores(): lax.dot_general(left, right, (((1,), (1,)), ((), ())), preferred_element_...  9.56 us
    all_to_all x1, blocking collectives, body(): lax.all_to_all(back, ('blk', 'split'), split_axis=0, concat_axis=0, tiled...  9.41 us
    all_to_all x1, starting transfers between devices, body(): lax.all_to_all(labels, ('blk', 'split'), split_axis=0, concat_axis=0, til...  7.41 us
    all_to_all x1, starting transfers between devices, body(): lax.all_to_all(packed, ('blk', 'split'), split_axis=0, concat_axis=0, til...  5.53 us
    gather x1, local copies, waits for them, and re-layouts, body(): packed = unit[order].reshape(count, piece, width)  5.21 us
    sort x1, other arithmetic, body(): order = jnp.argsort(target_pos)  5.12 us
  transfers between devices with their start and end apart: 15, of which 7 were waited for; matrix products, arithmetic and copies ran while one was open for 15% of the time, Pallas kernels for 0%

commit v1 on v0

--- a/solution.py
+++ b/solution.py
@@ -5,6 +5,28 @@
 
 MOST = 4096
 FILL = -4.0
+
+
+def cut_along(x, dim, size):
+    before, after = (x.shape[:dim], x.shape[dim + 1 :])
+    return jnp.moveaxis(x.reshape(*before, size, -1, *after), dim, 0)
+
+
+def joined_along(pieces, dim):
+    pieces = jnp.moveaxis(pieces, 0, dim)
+    dims = pieces.shape
+    return pieces.reshape(*dims[:dim], dims[dim] * dims[dim + 1], *dims[dim + 2 :])
+
+
+def exchange_in_pairs(value, axis, split_dim, concat_dim):
+    count, index = (lax.axis_size(axis), lax.axis_index(axis))
+    parts = cut_along(value, split_dim, count)
+    gathered = [parts[index]]
+    for step in range(1, count):
+        sent = parts[index ^ step]
+        gathered.append(lax.ppermute(sent, axis, [(i, i ^ step) for i in range(count)]))
+    parts = jnp.stack(gathered)[index ^ jnp.arange(count)]
+    return joined_along(parts, concat_dim)
 
 
 def from_behind(block, axis, distance):
@@ -76,9 +98,7 @@
     returned_home = from_behind(visit_best, ("blk", "split"), -reach)
     best = jnp.maximum(best, returned_home)
     back = best[local].reshape(count, piece)
-    returned = lax.all_to_all(
-        back, ("blk", "split"), split_axis=0, concat_axis=0, tiled=True
-    ).reshape(rows)
+    returned = exchange_in_pairs(back, ("blk", "split"), 0, 0).reshape(rows)
     return jnp.zeros((rows,), jnp.float32).at[order].set(returned)
 
 

time: 204 us -> 217 us (1.064)
  starting transfers between devices: 17.1 us -> 37.5 us
  blocking collectives: 9.41 us -> 0 us
    ppermute x0 -> x15, starting transfers between devices: none -> 20.5 us  [exchange_in_pairs(): lax.ppermute(sent, axis, [(i, i ^ step) for i in range(count)])]
    all_to_all x1 -> x0, blocking collectives: 9.41 us -> none  [body(): lax.all_to_all(back, ('blk', 'split'), split_axis=0, concat_axis=0, tiled...]
    ppermute x0 -> x15, waiting for transfers between devices: none -> 2.56 us  [exchange_in_pairs(): lax.ppermute(sent, axis, [(i, i ^ step) for i in range(count)])]
  transfers between devices with their start and end apart: 15 -> 30, of which waited for: 7 -> 9; matrix products, arithmetic and copies ran while one was open for 15% -> 14% of each run, Pallas kernels for 0% -> 0%
where the time goes in v1:
time: 217 us
  waiting for transfers between devices  117 us (54%)
  local copies, waits for them, and re-layouts  40.9 us (19%)
  starting transfers between devices  37.5 us (17%)
  other arithmetic  11.7 us (5%)
  matrix products  9.56 us (4%)
    ppermute x13, waiting for transfers between devices, from_behind(): return lax.ppermute(block, axis, route)  93.9 us
    ppermute x15, starting transfers between devices, exchange_in_pairs(): lax.ppermute(sent, axis, [(i, i ^ step) for i in range(count)])  20.5 us
    all_to_all x1, waiting for transfers between devices, body(): lax.all_to_all(packed, ('blk', 'split'), split_axis=0, concat_axis=0, til...  20.1 us
    dot_general x5, matrix products, masked_scores(): lax.dot_general(left, right, (((1,), (1,)), ((), ())), preferred_element_...  9.56 us
    all_to_all x1, starting transfers between devices, body(): lax.all_to_all(labels, ('blk', 'split'), split_axis=0, concat_axis=0, til...  7.41 us
    all_to_all x1, starting transfers between devices, body(): lax.all_to_all(packed, ('blk', 'split'), split_axis=0, concat_axis=0, til...  5.53 us
    gather x1, local copies, waits for them, and re-layouts, body(): packed = unit[order].reshape(count, piece, width)  5.21 us
    sort x1, other arithmetic, body(): order = jnp.argsort(target_pos)  5.12 us
  transfers between devices with their start and end apart: 30, of which 9 were waited for; matrix products, arithmetic and copies ran while one was open for 14% of the time, Pallas kernels for 0%

profile of v1, /device:TPU:0, one launch (start us, length us, event | category | flops | bytes accessed | tf_op | source)
XLA Modules:
  0.0 217.2 jit_solution(9462251945800347801)
XLA Ops:
  0.0 5.1 %sort.31 = (s32[1024]{0:T(1024)}, s32[1024]{0:T(1024)S(1)}) sort(s32[1024]{0:T(1024)} %param.7, s32[1024]{0:T(1024)S(1)} %iota.19), dimensions={0}, to_apply=%region_0.0 | sort | flops 10240 | bytes 16384 | tf_op jit(solution)/shard_map/jit(argsort)/sort | solution.py:54
  5.1 4.5 %gather_fusion.1 = s32[1024]{0:T(1024)S(1)} fusion(s32[1024]{0:T(1024)S(1)} %copy-done.1, s32[1024]{0:T(1024)S(1)} %get-tuple-element.108), kind=kCustom, calls=%fused_computation.1 | custom fusion | bytes 12288 | tf_op jit(solution)/shard_map/gather | solution.py:57
  9.8 4.5 %gather_fusion = s32[1024]{0:T(1024)S(1)} fusion(s32[1024]{0:T(1024)S(1)} %copy-done, s32[1024]{0:T(1024)S(1)} %get-tuple-element.108), kind=kCustom, calls=%fused_computation | custom fusion | bytes 12288 | tf_op jit(solution)/shard_map/gather | solution.py:57
  15.1 7.4 %all-to-all-start = ((s32[16,1,128]{2,1,0:T(1,128)}), s32[16,1,128]{2,1,0:T(1,128)S(1)}, u32[]{:S(2)}, u32[]{:S(2)}) async-start(s32[16,1,128]{2,1,0:T(1,128)} %reshape.149), calls=%async_computation | async-start | bytes 16384 | tf_op jit(solution)/shard_map/all_to_all | solution.py:61
  23.2 5.2 %gather_fusion.3 = bf16[1024,768]{1,0:T(8,128)(2,1)} fusion(bf16[1024,768]{1,0:T(8,128)(2,1)S(1)} %fusion.3, s32[1024]{0:T(1024)S(1)} %get-tuple-element.108), kind=kCustom, calls=%fused_computation.3 | custom fusion | bytes 3149824 | tf_op jit(solution)/shard_map/gather | solution.py:55
  28.9 5.5 %all-to-all-start.1 = ((bf16[16,64,768]{2,1,0:T(8,128)(2,1)}), bf16[16,64,768]{2,1,0:T(8,128)(2,1)S(1)}, u32[]{:S(2)}, u32[]{:S(2)}) async-start(bf16[16,64,768]{2,1,0:T(8,128)(2,1)} %bitcast), calls=%async_computation.1 | async-start | bytes 3145728 | tf_op jit(solution)/shard_map/all_to_all | solution.py:60
  37.2 4.4 %sort.32 = (s32[1024]{0:T(1024)}, s32[1024]{0:T(1024)S(1)}) sort(s32[1024]{0:T(1024)S(1)} %sub.21, s32[1024]{0:T(1024)S(1)} %iota.20), dimensions={0}, to_apply=%region_1.0 | sort | flops 10240 | bytes 16384 | tf_op jit(solution)/shard_map/jit(argsort)/sort | solution.py:66
  41.6 4.5 %gather_fusion.2 = s32[1024]{0:T(1024)S(1)} fusion(s32[1024]{0:T(1024)S(1)} %reshape_squeeze.4, s32[1024]{0:T(1024)S(1)} %fusion.4), kind=kCustom, calls=%fused_computation.2 | custom fusion | bytes 12288 | tf_op jit(solution)/shard_map/gather | solution.py:68
  46.2 20.1 %all-to-all-done.1 = bf16[16,64,768]{2,1,0:T(8,128)(2,1)S(1)} async-done(((bf16[16,64,768]{2,1,0:T(8,128)(2,1)}), bf16[16,64,768]{2,1,0:T(8,128)(2,1)S(1)}, u32[]{:S(2)}, u32[]{:S(2)}) %all-to-all-start.1) | async-done | bytes 1572896 | tf_op jit(solution)/shard_map/all_to_all | solution.py:60
  66.3 4.0 %gather_fusion.4 = bf16[1024,768]{1,0:T(8,128)(2,1)S(1)} fusion(bf16[1024,768]{1,0:T(8,128)(2,1)S(1)} %bitcast.90, s32[1024]{0:T(1024)S(1)} %fusion.4), kind=kCustom, calls=%fused_computation.4 | custom fusion | bytes 3149824 | tf_op jit(solution)/shard_map/gather | solution.py:67
  70.3 1.8 select_reduce_fusion
  73.3 107.0 %while.17 = (s32[]{:T(128)}, f32[1024]{0:T(1024)S(1)}, bf16[1024,768]{1,0:T(8,128)(2,1)}, s32[1024]{0:T(1024)S(1)}, f32[1024]{0:T(1024)S(1)}, /*index=5*/s32[102...) while((s32[]{:T(128)}, f32[1024]{0:T(1024)S(1)}, bf16[1024,768]{1,0:T(8,128)(2,1)}, ...), condition=%wide.region_7.8_spmd.clone, body=%wide.region_4.0_spmd.clone.sunk | while | flops 1614809088 | bytes 12660959 | solution.py:95
  74.3 1.8 collective-permute-start
  77.1 22.3 %collective-permute-done = s32[1024]{0:T(1024)S(1)} collective-permute-done((s32[1024]{0:T(1024)S(1)}, s32[1024]{0:T(1024)S(1)}, u32[]{:S(2)}, u32[]{:S(2)}) %collective-permute-start) | collective-permute-done | bytes 4128 | tf_op jit(solution)/shard_map/while/body/eval_jaxpr/ppermute | solution.py:35
  99.4 1.9 fusion.33
  102.7 22.6 %collective-permute-done = s32[1024]{0:T(1024)S(1)} collective-permute-done((s32[1024]{0:T(1024)S(1)}, s32[1024]{0:T(1024)S(1)}, u32[]{:S(2)}, u32[]{:S(2)}) %collective-permute-start) | collective-permute-done | bytes 4128 | tf_op jit(solution)/shard_map/while/body/eval_jaxpr/ppermute | solution.py:35
  125.3 1.9 fusion.33
  128.6 22.6 %collective-permute-done = s32[1024]{0:T(1024)S(1)} collective-permute-done((s32[1024]{0:T(1024)S(1)}, s32[1024]{0:T(1024)S(1)}, u32[]{:S(2)}, u32[]{:S(2)}) %collective-permute-start) | collective-permute-done | bytes 4128 | tf_op jit(solution)/shard_map/while/body/eval_jaxpr/ppermute | solution.py:35
  151.2 1.9 fusion.33
  154.5 22.7 %collective-permute-done = s32[1024]{0:T(1024)S(1)} collective-permute-done((s32[1024]{0:T(1024)S(1)}, s32[1024]{0:T(1024)S(1)}, u32[]{:S(2)}, u32[]{:S(2)}) %collective-permute-start) | collective-permute-done | bytes 4128 | tf_op jit(solution)/shard_map/while/body/eval_jaxpr/ppermute | solution.py:35
  177.2 1.9 fusion.33
  180.3 3.6 %collective-permute-done.3 = f32[1024]{0:T(1024)S(1)} collective-permute-done((f32[1024]{0:T(1024)S(1)}, f32[1024]{0:T(1024)S(1)}, u32[]{:S(2)}, u32[]{:S(2)}) %collective-permute-start.3) | collective-permute-done | bytes 4128 | tf_op jit(solution)/shard_map/ppermute | solution.py:35
  183.9 4.5 %gather_fusion.5 = f32[1024]{0:T(1024)S(1)} fusion(f32[1024]{0:T(1024)S(1)} %max.9, s32[1024]{0:T(1024)S(1)} %broadcast_clamp_fusion), kind=kCustom, calls=%fused_computation.5 | custom fusion | bytes 12288 | tf_op jit(solution)/shard_map/gather | solution.py:100
  188.7 1.8 collective-permute-start.6
  190.5 1.7 collective-permute-start.8
  192.3 2.6 %collective-permute-start.10 = (f32[1,64]{1,0:T(1,128)S(1)}, f32[1,64]{1,0:T(1,128)S(1)}, u32[]{:S(2)}, u32[]{:S(2)}) collective-permute-start(f32[1,64]{1,0:T(1,128)S(1)} %get-tuple-element.100), channel_id=1, source_target_pairs={{0,7},{1,6},{2,5},{3,4},{4,3},{5,2},{6,1},{7,0},{8,15},{9,14},{10,... | collective-permute-start | bytes 776 | tf_op jit(solution)/shard_map/ppermute | solution.py:27
  195.2 2.3 %collective-permute-start.12 = (f32[1,64]{1,0:T(1,128)S(1)}, f32[1,64]{1,0:T(1,128)S(1)}, u32[]{:S(2)}, u32[]{:S(2)}) collective-permute-start(f32[1,64]{1,0:T(1,128)S(1)} %get-tuple-element.98), channel_id=1, source_target_pairs={{0,9},{1,8},{2,11},{3,10},{4,13},{5,12},{6,15},{7,14},{8,1},{9,0},... | collective-permute-start | bytes 776 | tf_op jit(solution)/shard_map/ppermute | solution.py:27
  198.0 3.1 %collective-permute-start.14 = (f32[1,64]{1,0:T(1,128)S(1)}, f32[1,64]{1,0:T(1,128)S(1)}, u32[]{:S(2)}, u32[]{:S(2)}) collective-permute-start(f32[1,64]{1,0:T(1,128)S(1)} %get-tuple-element.96), channel_id=1, source_target_pairs={{0,11},{1,10},{2,9},{3,8},{4,15},{5,14},{6,13},{7,12},{8,3},{9,2},... | collective-permute-start | bytes 776 | tf_op jit(solution)/shard_map/ppermute | solution.py:27
  201.1 1.8 collective-permute-start.15
  205.9 3.2 %collective-permute-start.18 = (f32[1,64]{1,0:T(1,128)S(1)}, f32[1,64]{1,0:T(1,128)S(1)}, u32[]{:S(2)}, u32[]{:S(2)}) collective-permute-start(f32[1,64]{1,0:T(1,128)S(1)} %get-tuple-element.92), channel_id=1, source_target_pairs={{0,15},{1,14},{2,13},{3,12},{4,11},{5,10},{6,9},{7,8},{8,7},{9,6},... | collective-permute-start | bytes 776 | tf_op jit(solution)/shard_map/ppermute | solution.py:27
  209.1 1.7 collective-permute-done.17
  212.3 4.9 %scatter_custom_fusion = f32[1024]{0:T(1024)} fusion(s32[1024]{0:T(1024)S(1)} %get-tuple-element.109, f32[1024]{0:T(1024)S(1)} %reshape.119, f32[]{:T(128)} %constant.32.clone.1), kind=kCustom, calls=%fused_computation.47 | custom fusion | bytes 4100 | tf_op jit(solution)/shard_map/scatter | solution.py:102
  (101 shorter events, 18.5 us)
Async XLA Ops:
  0.0 9.8 %copy-start = (s32[1024]{0:T(1024)S(1)}, s32[1024]{0:T(1024)}, u32[]{:S(2)}) copy-start(s32[1024]{0:T(1024)} %param.6) | copy-start | bytes 12292
  9.8 12.7 %copy-start.2 = (bf16[1024,768]{1,0:T(8,128)(2,1)S(1)}, bf16[1024,768]{1,0:T(8,128)(2,1)}, u32[]{:S(2)}) copy-start(bf16[1024,768]{1,0:T(8,128)(2,1)} %param.5) | copy-start | bytes 4718596
  15.1 13.8 %all-to-all-start = ((s32[16,1,128]{2,1,0:T(1,128)}), s32[16,1,128]{2,1,0:T(1,128)S(1)}, u32[]{:S(2)}, u32[]{:S(2)}) async-start(s32[16,1,128]{2,1,0:T(1,128)} %reshape.149), calls=%async_computation | async-start | bytes 16384 | tf_op jit(solution)/shard_map/all_to_all | solution.py:61
  28.9 37.4 %all-to-all-start.1 = ((bf16[16,64,768]{2,1,0:T(8,128)(2,1)}), bf16[16,64,768]{2,1,0:T(8,128)(2,1)S(1)}, u32[]{:S(2)}, u32[]{:S(2)}) async-start(bf16[16,64,768]{2,1,0:T(8,128)(2,1)} %bitcast), calls=%async_computation.1 | async-start | bytes 3145728 | tf_op jit(solution)/shard_map/all_to_all | solution.py:60
  73.3 26.1 %collective-permute-start.1 = (bf16[1024,768]{1,0:T(8,128)(2,1)}, bf16[1024,768]{1,0:T(8,128)(2,1)S(1)}, u32[]{:S(2)}, u32[]{:S(2)}) collective-permute-start(bf16[1024,768]{1,0:T(8,128)(2,1)} %get-tuple-element.168), channel_id=1, source_target_pairs={{15,0},{0,1},{1,2},{2,3},{3,4},{4,5},{5,6},{6,7},{7,8},{8,9},{9,10... | collective-permute-start | bytes 4718600 | tf_op jit(solution)/shard_map/while/body/eval_jaxpr/ppermute | solution.py:35
  74.3 25.1 %collective-permute-start = (s32[1024]{0:T(1024)S(1)}, s32[1024]{0:T(1024)S(1)}, u32[]{:S(2)}, u32[]{:S(2)}) collective-permute-start(s32[1024]{0:T(1024)S(1)} %get-tuple-element.169), channel_id=1, source_target_pairs={{15,0},{0,1},{1,2},{2,3},{3,4},{4,5},{5,6},{6,7},{7,8},{8,9},{9,10... | collective-permute-start | bytes 12296 | tf_op jit(solution)/shard_map/while/body/eval_jaxpr/ppermute | solution.py:35
  76.1 26.4 %collective-permute-start.2 = (bf16[1024]{0:T(1024)(128)(2,1)S(1)}, bf16[1024]{0:T(1024)(128)(2,1)S(1)}, u32[]{:S(2)}, u32[]{:S(2)}) collective-permute-start(bf16[1024]{0:T(1024)(128)(2,1)S(1)} %select_convert_fusion.2), channel_id=1, source_target_pairs={{15,0},{0,1},{1,2},{2,3},{3,4},{4,5},{5,6},{6,7},{7,8},{8,9},{9,10... | collective-permute-start | bytes 6152 | tf_op jit(solution)/shard_map/while/body/eval_jaxpr/ppermute | solution.py:35
  102.5 22.8 %collective-permute-start.1 = (bf16[1024,768]{1,0:T(8,128)(2,1)}, bf16[1024,768]{1,0:T(8,128)(2,1)S(1)}, u32[]{:S(2)}, u32[]{:S(2)}) collective-permute-start(bf16[1024,768]{1,0:T(8,128)(2,1)} %get-tuple-element.168), channel_id=1, source_target_pairs={{15,0},{0,1},{1,2},{2,3},{3,4},{4,5},{5,6},{6,7},{7,8},{8,9},{9,10... | collective-permute-start | bytes 4718600 | tf_op jit(solution)/shard_map/while/body/eval_jaxpr/ppermute | solution.py:35
  102.5 22.8 %collective-permute-start = (s32[1024]{0:T(1024)S(1)}, s32[1024]{0:T(1024)S(1)}, u32[]{:S(2)}, u32[]{:S(2)}) collective-permute-start(s32[1024]{0:T(1024)S(1)} %get-tuple-element.169), channel_id=1, source_target_pairs={{15,0},{0,1},{1,2},{2,3},{3,4},{4,5},{5,6},{6,7},{7,8},{8,9},{9,10... | collective-permute-start | bytes 12296 | tf_op jit(solution)/shard_map/while/body/eval_jaxpr/ppermute | solution.py:35
  102.6 25.8 %collective-permute-start.2 = (bf16[1024]{0:T(1024)(128)(2,1)S(1)}, bf16[1024]{0:T(1024)(128)(2,1)S(1)}, u32[]{:S(2)}, u32[]{:S(2)}) collective-permute-start(bf16[1024]{0:T(1024)(128)(2,1)S(1)} %select_convert_fusion.2), channel_id=1, source_target_pairs={{15,0},{0,1},{1,2},{2,3},{3,4},{4,5},{5,6},{6,7},{7,8},{8,9},{9,10... | collective-permute-start | bytes 6152 | tf_op jit(solution)/shard_map/while/body/eval_jaxpr/ppermute | solution.py:35
  128.4 22.8 %collective-permute-start.1 = (bf16[1024,768]{1,0:T(8,128)(2,1)}, bf16[1024,768]{1,0:T(8,128)(2,1)S(1)}, u32[]{:S(2)}, u32[]{:S(2)}) collective-permute-start(bf16[1024,768]{1,0:T(8,128)(2,1)} %get-tuple-element.168), channel_id=1, source_target_pairs={{15,0},{0,1},{1,2},{2,3},{3,4},{4,5},{5,6},{6,7},{7,8},{8,9},{9,10... | collective-permute-start | bytes 4718600 | tf_op jit(solution)/shard_map/while/body/eval_jaxpr/ppermute | solution.py:35
  128.4 22.8 %collective-permute-start = (s32[1024]{0:T(1024)S(1)}, s32[1024]{0:T(1024)S(1)}, u32[]{:S(2)}, u32[]{:S(2)}) collective-permute-start(s32[1024]{0:T(1024)S(1)} %get-tuple-element.169), channel_id=1, source_target_pairs={{15,0},{0,1},{1,2},{2,3},{3,4},{4,5},{5,6},{6,7},{7,8},{8,9},{9,10... | collective-permute-start | bytes 12296 | tf_op jit(solution)/shard_map/while/body/eval_jaxpr/ppermute | solution.py:35
  128.5 25.8 %collective-permute-start.2 = (bf16[1024]{0:T(1024)(128)(2,1)S(1)}, bf16[1024]{0:T(1024)(128)(2,1)S(1)}, u32[]{:S(2)}, u32[]{:S(2)}) collective-permute-start(bf16[1024]{0:T(1024)(128)(2,1)S(1)} %select_convert_fusion.2), channel_id=1, source_target_pairs={{15,0},{0,1},{1,2},{2,3},{3,4},{4,5},{5,6},{6,7},{7,8},{8,9},{9,10... | collective-permute-start | bytes 6152 | tf_op jit(solution)/shard_map/while/body/eval_jaxpr/ppermute | solution.py:35
  154.3 22.9 %collective-permute-start.1 = (bf16[1024,768]{1,0:T(8,128)(2,1)}, bf16[1024,768]{1,0:T(8,128)(2,1)S(1)}, u32[]{:S(2)}, u32[]{:S(2)}) collective-permute-start(bf16[1024,768]{1,0:T(8,128)(2,1)} %get-tuple-element.168), channel_id=1, source_target_pairs={{15,0},{0,1},{1,2},{2,3},{3,4},{4,5},{5,6},{6,7},{7,8},{8,9},{9,10... | collective-permute-start | bytes 4718600 | tf_op jit(solution)/shard_map/while/body/eval_jaxpr/ppermute | solution.py:35
  154.3 22.9 %collective-permute-start = (s32[1024]{0:T(1024)S(1)}, s32[1024]{0:T(1024)S(1)}, u32[]{:S(2)}, u32[]{:S(2)}) collective-permute-start(s32[1024]{0:T(1024)S(1)} %get-tuple-element.169), channel_id=1, source_target_pairs={{15,0},{0,1},{1,2},{2,3},{3,4},{4,5},{5,6},{6,7},{7,8},{8,9},{9,10... | collective-permute-start | bytes 12296 | tf_op jit(solution)/shard_map/while/body/eval_jaxpr/ppermute | solution.py:35
  154.4 25.9 %collective-permute-start.2 = (bf16[1024]{0:T(1024)(128)(2,1)S(1)}, bf16[1024]{0:T(1024)(128)(2,1)S(1)}, u32[]{:S(2)}, u32[]{:S(2)}) collective-permute-start(bf16[1024]{0:T(1024)(128)(2,1)S(1)} %select_convert_fusion.2), channel_id=1, source_target_pairs={{15,0},{0,1},{1,2},{2,3},{3,4},{4,5},{5,6},{6,7},{7,8},{8,9},{9,10... | collective-permute-start | bytes 6152 | tf_op jit(solution)/shard_map/while/body/eval_jaxpr/ppermute | solution.py:35
  180.3 3.6 %collective-permute-start.3 = (f32[1024]{0:T(1024)S(1)}, f32[1024]{0:T(1024)S(1)}, u32[]{:S(2)}, u32[]{:S(2)}) collective-permute-start(f32[1024]{0:T(1024)S(1)} %get-tuple-element.48), channel_id=1, source_target_pairs={{4,0},{5,1},{6,2},{7,3},{8,4},{9,5},{10,6},{11,7},{12,8},{13,9},{1... | collective-permute-start | bytes 12296 | tf_op jit(solution)/shard_map/ppermute | solution.py:35
  188.6 3.6 %collective-permute-start.4 = (f32[1,64]{1,0:T(1,128)S(1)}, f32[1,64]{1,0:T(1,128)S(1)}, u32[]{:S(2)}, u32[]{:S(2)}) collective-permute-start(f32[1,64]{1,0:T(1,128)S(1)} %get-tuple-element.106), channel_id=1, source_target_pairs={{0,1},{1,0},{2,3},{3,2},{4,5},{5,4},{6,7},{7,6},{8,9},{9,8},{10,11... | collective-permute-start | bytes 776 | tf_op jit(solution)/shard_map/ppermute | solution.py:27
  188.7 3.6 %collective-permute-start.5 = (f32[1,64]{1,0:T(1,128)S(1)}, f32[1,64]{1,0:T(1,128)S(1)}, u32[]{:S(2)}, u32[]{:S(2)}) collective-permute-start(f32[1,64]{1,0:T(1,128)S(1)} %get-tuple-element.105), channel_id=1, source_target_pairs={{0,2},{1,3},{2,0},{3,1},{4,6},{5,7},{6,4},{7,5},{8,10},{9,11},{10,... | collective-permute-start | bytes 776 | tf_op jit(solution)/shard_map/ppermute | solution.py:27
  188.7 6.2 %collective-permute-start.6 = (f32[1,64]{1,0:T(1,128)S(1)}, f32[1,64]{1,0:T(1,128)S(1)}, u32[]{:S(2)}, u32[]{:S(2)}) collective-permute-start(f32[1,64]{1,0:T(1,128)S(1)} %get-tuple-element.104), channel_id=1, source_target_pairs={{0,3},{1,2},{2,1},{3,0},{4,7},{5,6},{6,5},{7,4},{8,11},{9,10},{10,... | collective-permute-start | bytes 776 | tf_op jit(solution)/shard_map/ppermute | solution.py:27
  190.5 4.7 %collective-permute-start.7 = (f32[1,64]{1,0:T(1,128)S(1)}, f32[1,64]{1,0:T(1,128)S(1)}, u32[]{:S(2)}, u32[]{:S(2)}) collective-permute-start(f32[1,64]{1,0:T(1,128)S(1)} %get-tuple-element.103), channel_id=1, source_target_pairs={{0,4},{1,5},{2,6},{3,7},{4,0},{5,1},{6,2},{7,3},{8,12},{9,13},{10,... | collective-permute-start | bytes 776 | tf_op jit(solution)/shard_map/ppermute | solution.py:27
  190.5 7.0 %collective-permute-start.8 = (f32[1,64]{1,0:T(1,128)S(1)}, f32[1,64]{1,0:T(1,128)S(1)}, u32[]{:S(2)}, u32[]{:S(2)}) collective-permute-start(f32[1,64]{1,0:T(1,128)S(1)} %get-tuple-element.102), channel_id=1, source_target_pairs={{0,5},{1,4},{2,7},{3,6},{4,1},{5,0},{6,3},{7,2},{8,13},{9,12},{10,... | collective-permute-start | bytes 776 | tf_op jit(solution)/shard_map/ppermute | solution.py:27
  192.2 5.8 %collective-permute-start.9 = (f32[1,64]{1,0:T(1,128)S(1)}, f32[1,64]{1,0:T(1,128)S(1)}, u32[]{:S(2)}, u32[]{:S(2)}) collective-permute-start(f32[1,64]{1,0:T(1,128)S(1)} %get-tuple-element.101), channel_id=1, source_target_pairs={{0,6},{1,7},{2,4},{3,5},{4,2},{5,3},{6,0},{7,1},{8,14},{9,15},{10,... | collective-permute-start | bytes 776 | tf_op jit(solution)/shard_map/ppermute | solution.py:27
  192.3 8.8 %collective-permute-start.10 = (f32[1,64]{1,0:T(1,128)S(1)}, f32[1,64]{1,0:T(1,128)S(1)}, u32[]{:S(2)}, u32[]{:S(2)}) collective-permute-start(f32[1,64]{1,0:T(1,128)S(1)} %get-tuple-element.100), channel_id=1, source_target_pairs={{0,7},{1,6},{2,5},{3,4},{4,3},{5,2},{6,1},{7,0},{8,15},{9,14},{10,... | collective-permute-start | bytes 776 | tf_op jit(solution)/shard_map/ppermute | solution.py:27
  194.9 8.0 %collective-permute-start.11 = (f32[1,64]{1,0:T(1,128)S(1)}, f32[1,64]{1,0:T(1,128)S(1)}, u32[]{:S(2)}, u32[]{:S(2)}) collective-permute-start(f32[1,64]{1,0:T(1,128)S(1)} %get-tuple-element.99), channel_id=1, source_target_pairs={{0,8},{1,9},{2,10},{3,11},{4,12},{5,13},{6,14},{7,15},{8,0},{9,1},... | collective-permute-start | bytes 776 | tf_op jit(solution)/shard_map/ppermute | solution.py:27
  195.2 9.4 %collective-permute-start.12 = (f32[1,64]{1,0:T(1,128)S(1)}, f32[1,64]{1,0:T(1,128)S(1)}, u32[]{:S(2)}, u32[]{:S(2)}) collective-permute-start(f32[1,64]{1,0:T(1,128)S(1)} %get-tuple-element.98), channel_id=1, source_target_pairs={{0,9},{1,8},{2,11},{3,10},{4,13},{5,12},{6,15},{7,14},{8,1},{9,0},... | collective-permute-start | bytes 776 | tf_op jit(solution)/shard_map/ppermute | solution.py:27
  197.5 8.4 %collective-permute-start.13 = (f32[1,64]{1,0:T(1,128)S(1)}, f32[1,64]{1,0:T(1,128)S(1)}, u32[]{:S(2)}, u32[]{:S(2)}) collective-permute-start(f32[1,64]{1,0:T(1,128)S(1)} %get-tuple-element.97), channel_id=1, source_target_pairs={{0,10},{1,11},{2,8},{3,9},{4,14},{5,15},{6,12},{7,13},{8,2},{9,3},... | collective-permute-start | bytes 776 | tf_op jit(solution)/shard_map/ppermute | solution.py:27
  198.0 11.1 %collective-permute-start.14 = (f32[1,64]{1,0:T(1,128)S(1)}, f32[1,64]{1,0:T(1,128)S(1)}, u32[]{:S(2)}, u32[]{:S(2)}) collective-permute-start(f32[1,64]{1,0:T(1,128)S(1)} %get-tuple-element.96), channel_id=1, source_target_pairs={{0,11},{1,10},{2,9},{3,8},{4,15},{5,14},{6,13},{7,12},{8,3},{9,2},... | collective-permute-start | bytes 776 | tf_op jit(solution)/shard_map/ppermute | solution.py:27
  201.1 8.0 %collective-permute-start.15 = (f32[1,64]{1,0:T(1,128)S(1)}, f32[1,64]{1,0:T(1,128)S(1)}, u32[]{:S(2)}, u32[]{:S(2)}) collective-permute-start(f32[1,64]{1,0:T(1,128)S(1)} %get-tuple-element.95), channel_id=1, source_target_pairs={{0,12},{1,13},{2,14},{3,15},{4,8},{5,9},{6,10},{7,11},{8,4},{9,5},... | collective-permute-start | bytes 776 | tf_op jit(solution)/shard_map/ppermute | solution.py:27
  202.9 6.2 %collective-permute-start.16 = (f32[1,64]{1,0:T(1,128)S(1)}, f32[1,64]{1,0:T(1,128)S(1)}, u32[]{:S(2)}, u32[]{:S(2)}) collective-permute-start(f32[1,64]{1,0:T(1,128)S(1)} %get-tuple-element.94), channel_id=1, source_target_pairs={{0,13},{1,12},{2,15},{3,14},{4,9},{5,8},{6,11},{7,10},{8,5},{9,4},... | collective-permute-start | bytes 776 | tf_op jit(solution)/shard_map/ppermute | solution.py:27
  204.6 6.3 %collective-permute-start.17 = (f32[1,64]{1,0:T(1,128)S(1)}, f32[1,64]{1,0:T(1,128)S(1)}, u32[]{:S(2)}, u32[]{:S(2)}) collective-permute-start(f32[1,64]{1,0:T(1,128)S(1)} %get-tuple-element.93), channel_id=1, source_target_pairs={{0,14},{1,15},{2,12},{3,13},{4,10},{5,11},{6,8},{7,9},{8,6},{9,7},... | collective-permute-start | bytes 776 | tf_op jit(solution)/shard_map/ppermute | solution.py:27
  205.9 5.7 %collective-permute-start.18 = (f32[1,64]{1,0:T(1,128)S(1)}, f32[1,64]{1,0:T(1,128)S(1)}, u32[]{:S(2)}, u32[]{:S(2)}) collective-permute-start(f32[1,64]{1,0:T(1,128)S(1)} %get-tuple-element.92), channel_id=1, source_target_pairs={{0,15},{1,14},{2,13},{3,12},{4,11},{5,10},{6,9},{7,8},{8,7},{9,6},... | collective-permute-start | bytes 776 | tf_op jit(solution)/shard_map/ppermute | solution.py:27
  (1 other events, 5.1 us)
